TPU v7x, 32 devices: a whole 2x2x4 slice. The times are simulated.
32 devices in a mesh: seq: 16 (over z, x, core), batch: 2 (over y).
Axes of the slice: x: 2, y: 2, z: 4, core: 2. Of those that a mesh axis runs over, the one named last changes fastest.
Arguments:
- inputs: bfloat16 [2, 4096, 1024], P('batch', 'seq'), may hold values from -6 to 6
- grad_out: bfloat16 [2, 4096, 1024], P('batch', 'seq'), may hold values from -6 to 6
- spectrum: float32 [2, 32, 256, 1024], P(None, 'seq', None, 'batch'), may hold values from -6 to 6
- first_moment: float32 [2, 32, 256, 1024], P(None, 'seq', None, 'batch'), may hold values from -2 to 2
- second_moment: float32 [2, 32, 256, 1024], P(None, 'seq', None, 'batch'), may hold values from 0.1 to 4
Outputs:
- new_spectrum: float32 [2, 32, 256, 1024], P(None, 'seq', None, 'batch')
- new_first: float32 [2, 32, 256, 1024], P(None, 'seq', None, 'batch')
- new_second: float32 [2, 32, 256, 1024], P(None, 'seq', None, 'batch')
- filtered: bfloat16 [2, 4096, 1024], P('batch', 'seq')
All inputs are finite; a program needn't handle non-finite values.
Results may differ from a plain program's by a relative error of at most 0.0055.
Values may be sent and summed in bfloat16 or wider, within the bound.
No kernel may reach another device: no remote copies, remote signals or barrier semaphores. Data moves between devices by JAX's collectives and lax.ppermute only.
A program may use at most 64 MiB of HBM per device.

v0:
```python
import math
import jax
import jax.numpy as jnp
from jax import lax
from jax.sharding import PartitionSpec as P

full_turn = 2.0 * math.pi
step_rate = 0.5
epsilon = 1e-06


def angles(numer, modulus):
    return full_turn * (numer % modulus).astype(jnp.float32) / modulus


def phase_pair(first_count, second_count, modulus):
    first_index = jnp.arange(first_count, dtype=jnp.int32)
    second_index = jnp.arange(second_count, dtype=jnp.int32)
    phases = angles(first_index[:, None] * second_index[None, :], modulus)
    return (jnp.cos(phases), jnp.sin(phases))


def local_forward(sequence, seq_count, point_count):
    batch_rows = sequence.shape[0]
    outer_count = 2 * seq_count
    full_length = outer_count * point_count
    values = sequence.reshape(batch_rows, seq_count, point_count, -1).astype(jnp.float32)
    outer_cos, outer_sin = phase_pair(outer_count, seq_count, outer_count)
    real_one = jnp.einsum("ja,bach->bjch", outer_cos, values, precision=lax.Precision.HIGHEST)
    imag_one = -jnp.einsum("ja,bach->bjch", outer_sin, values, precision=lax.Precision.HIGHEST)
    twist_cos, twist_sin = phase_pair(outer_count, point_count, full_length)
    twist_cos = twist_cos[None, :, :, None]
    twist_sin = twist_sin[None, :, :, None]
    real_two = real_one * twist_cos + imag_one * twist_sin
    imag_two = imag_one * twist_cos - real_one * twist_sin
    inner_cos, inner_sin = phase_pair(point_count, point_count, point_count)
    real_out = jnp.einsum(
        "cm,bjch->bjmh", inner_cos, real_two, precision=lax.Precision.HIGHEST
    ) + jnp.einsum("cm,bjch->bjmh", inner_sin, imag_two, precision=lax.Precision.HIGHEST)
    imag_out = jnp.einsum(
        "cm,bjch->bjmh", inner_cos, imag_two, precision=lax.Precision.HIGHEST
    ) - jnp.einsum("cm,bjch->bjmh", inner_sin, real_two, precision=lax.Precision.HIGHEST)
    return (real_out, imag_out)


def local_inverse(real_in, imag_in, seq_count, point_count):
    outer_count = 2 * seq_count
    full_length = outer_count * point_count
    inner_cos, inner_sin = phase_pair(point_count, point_count, point_count)
    real_one = jnp.einsum(
        "mc,bjmh->bjch", inner_cos, real_in, precision=lax.Precision.HIGHEST
    ) - jnp.einsum("mc,bjmh->bjch", inner_sin, imag_in, precision=lax.Precision.HIGHEST)
    imag_one = jnp.einsum(
        "mc,bjmh->bjch", inner_sin, real_in, precision=lax.Precision.HIGHEST
    ) + jnp.einsum("mc,bjmh->bjch", inner_cos, imag_in, precision=lax.Precision.HIGHEST)
    twist_cos, twist_sin = phase_pair(outer_count, point_count, full_length)
    twist_cos = twist_cos[None, :, :, None]
    twist_sin = twist_sin[None, :, :, None]
    real_two = real_one * twist_cos - imag_one * twist_sin
    imag_two = real_one * twist_sin + imag_one * twist_cos
    outer_cos, outer_sin = phase_pair(outer_count, seq_count, outer_count)
    result = jnp.einsum(
        "ja,bjch->bach", outer_cos, real_two, precision=lax.Precision.HIGHEST
    ) - jnp.einsum("ja,bjch->bach", outer_sin, imag_two, precision=lax.Precision.HIGHEST)
    return result / full_length


def channel_layout(inputs, grad_out, spectrum, first_moment, second_moment):
    seq_count = lax.axis_size("seq")
    batch_count = lax.axis_size("batch")
    batch_rows, point_count, channels = inputs.shape
    narrow = channels // (seq_count * batch_count)
    group_width = batch_count * narrow
    outer_count = 2 * seq_count
    full_length = outer_count * point_count
    local_outer = spectrum.shape[1]
    signal_parts = inputs.reshape(batch_rows, point_count, batch_count, seq_count, narrow)
    cotangent_parts = grad_out.reshape(batch_rows, point_count, batch_count, seq_count, narrow)
    signal_cols, cotangent_cols = (
        lax.all_to_all(signal_parts, "seq", split_axis=3, concat_axis=1, tiled=True),
        lax.all_to_all(cotangent_parts, "seq", split_axis=3, concat_axis=1, tiled=True),
    )
    state_shape = (2, local_outer, point_count, seq_count, narrow)
    spec_cols, first_cols, second_cols = (
        lax.all_to_all(
            spectrum.reshape(state_shape), "seq", split_axis=3, concat_axis=1, tiled=True
        ),
        lax.all_to_all(
            first_moment.reshape(state_shape), "seq", split_axis=3, concat_axis=1, tiled=True
        ),
        lax.all_to_all(
            second_moment.reshape(state_shape), "seq", split_axis=3, concat_axis=1, tiled=True
        ),
    )
    own_shape = (2, outer_count, point_count, narrow)
    spec_cols = spec_cols.reshape(own_shape)
    first_cols = first_cols.reshape(own_shape)
    second_cols = second_cols.reshape(own_shape)
    signal_real, signal_imag = local_forward(
        signal_cols.reshape(batch_rows, seq_count * point_count, group_width),
        seq_count,
        point_count,
    )
    cotangent_real, cotangent_imag = local_forward(
        cotangent_cols.reshape(batch_rows, seq_count * point_count, group_width),
        seq_count,
        point_count,
    )
    real_term = jnp.sum(signal_real * cotangent_real + signal_imag * cotangent_imag, axis=0)
    imag_term = jnp.sum(signal_real * cotangent_imag - signal_imag * cotangent_real, axis=0)
    local_grad = (jnp.stack([real_term, imag_term]) / full_length).reshape(
        2, outer_count, point_count, batch_count, narrow
    )
    own_grad = (
        lax.psum_scatter(local_grad.astype(jnp.bfloat16), "batch", scatter_dimension=3, tiled=True)
        .astype(jnp.float32)
        .reshape(own_shape)
    )
    new_first = 0.9 * first_cols + 0.1 * own_grad
    new_second = 0.99 * second_cols + 0.01 * own_grad * own_grad
    new_spectrum = spec_cols - step_rate * jnp.tanh(new_first / (jnp.sqrt(new_second) + epsilon))
    group_filter = lax.all_gather(new_spectrum, "batch", axis=3, tiled=True)
    filter_real = group_filter[0][None]
    filter_imag = group_filter[1][None]
    mixed_real = signal_real * filter_real - signal_imag * filter_imag
    mixed_imag = signal_real * filter_imag + signal_imag * filter_real
    rows_back = local_inverse(mixed_real, mixed_imag, seq_count, point_count)
    rows_back = rows_back.astype(jnp.bfloat16).reshape(
        batch_rows, seq_count * point_count, batch_count, 1, narrow
    )
    back_shape = (2, outer_count, point_count, 1, narrow)
    spec_back, first_back, second_back = (
        lax.all_to_all(
            new_spectrum.reshape(back_shape), "seq", split_axis=1, concat_axis=3, tiled=True
        ),
        lax.all_to_all(
            new_first.reshape(back_shape), "seq", split_axis=1, concat_axis=3, tiled=True
        ),
        lax.all_to_all(
            new_second.reshape(back_shape), "seq", split_axis=1, concat_axis=3, tiled=True
        ),
    )
    filtered = lax.all_to_all(rows_back, "seq", split_axis=1, concat_axis=3, tiled=True)
    final_shape = spectrum.shape
    return (
        spec_back.reshape(final_shape),
        first_back.reshape(final_shape),
        second_back.reshape(final_shape),
        filtered.reshape(batch_rows, point_count, channels),
    )


def per_device(inputs, grad_out, spectrum, first_moment, second_moment):
    return channel_layout(inputs, grad_out, spectrum, first_moment, second_moment)


def solution(mesh):
    return jax.shard_map(
        per_device,
        mesh=mesh,
        in_specs=(
            P("batch", "seq", None),
            P("batch", "seq", None),
            P(None, "seq", None, "batch"),
            P(None, "seq", None, "batch"),
            P(None, "seq", None, "batch"),
        ),
        out_specs=(
            P(None, "seq", None, "batch"),
            P(None, "seq", None, "batch"),
            P(None, "seq", None, "batch"),
            P("batch", "seq", None),
        ),
        check_vma=False,
    )
```

profile of v0, /device:TPU:0, one launch (start us, length us, event | category | flops | bytes accessed | tf_op | source)
XLA Modules:
  0.0 404.6 jit_solution(18138972879335876599)
XLA Ops:
  9.3 7.4 %all-to-all-start.3 = ((bf16[1,256,2,16,32]{1,4,2,0,3:T(8,128)(2,1)}), bf16[1,256,2,16,32]{1,4,2,0,3:T(8,128)(2,1)S(1)}, u32[]{:S(2)}, u32[]{:S(2)}) async-start(bf16[1,256,2,16,32]{1,4,2,0,3:T(8,128)(2,1)} %copy.145), calls=%async_computation.3 | async-start | bytes 1048576 | tf_op jit(solution)/shard_map/all_to_all | solution.py:81
  17.8 13.2 %all-to-all-done.3 = bf16[1,256,2,16,32]{1,4,2,0,3:T(8,128)(2,1)S(1)} async-done(((bf16[1,256,2,16,32]{1,4,2,0,3:T(8,128)(2,1)}), bf16[1,256,2,16,32]{1,4,2,0,3:T(8,128)(2,1)S(1)}, u32[]{:S(2)}, u32[]{:S(2)}) %all-to-all-start.3) | async-done | bytes 524320 | tf_op jit(solution)/shard_map/all_to_all | solution.py:81
  31.0 4.2 %all-to-all-start.2 = ((bf16[1,256,2,16,32]{1,4,2,0,3:T(8,128)(2,1)}), bf16[1,256,2,16,32]{1,4,2,0,3:T(8,128)(2,1)S(1)}, u32[]{:S(2)}, u32[]{:S(2)}) async-start(bf16[1,256,2,16,32]{1,4,2,0,3:T(8,128)(2,1)} %copy.140), calls=%async_computation.2 | async-start | bytes 1048576 | tf_op jit(solution)/shard_map/all_to_all | solution.py:80
  38.6 10.8 %all-to-all-done.2 = bf16[1,256,2,16,32]{1,4,2,0,3:T(8,128)(2,1)S(1)} async-done(((bf16[1,256,2,16,32]{1,4,2,0,3:T(8,128)(2,1)}), bf16[1,256,2,16,32]{1,4,2,0,3:T(8,128)(2,1)S(1)}, u32[]{:S(2)}, u32[]{:S(2)}) %all-to-all-start.2) | async-done | bytes 524320 | tf_op jit(solution)/shard_map/all_to_all | solution.py:80
  49.4 4.2 %all-to-all-start.1 = ((f32[2,2,256,16,32]{2,4,1,0,3:T(8,128)}), f32[2,2,256,16,32]{2,4,1,0,3:T(8,128)S(1)}, u32[]{:S(2)}, u32[]{:S(2)}) async-start(f32[2,2,256,16,32]{2,4,1,0,3:T(8,128)} %copy.137), calls=%async_computation.1 | async-start | bytes 4194304 | tf_op jit(solution)/shard_map/all_to_all | solution.py:88
  53.6 2.9 copy.155
  56.5 3.2 copy.156
  60.4 2.5 fusion.132
  62.8 2.4 fusion.137
  65.3 2.4 fusion.134
  67.6 26.9 %all-to-all-done.1 = f32[2,2,256,16,32]{2,4,1,0,3:T(8,128)S(1)} async-done(((f32[2,2,256,16,32]{2,4,1,0,3:T(8,128)}), f32[2,2,256,16,32]{2,4,1,0,3:T(8,128)S(1)}, u32[]{:S(2)}, u32[]{:S(2)}) %all-to-all-start.1) | async-done | bytes 2097184 | tf_op jit(solution)/shard_map/all_to_all | solution.py:88
  95.9 11.3 %all-to-all-start.4 = ((f32[2,2,256,16,32]{2,4,1,0,3:T(8,128)}), f32[2,2,256,16,32]{2,4,1,0,3:T(8,128)}, u32[]{:S(2)}, u32[]{:S(2)}) async-start(f32[2,2,256,16,32]{2,4,1,0,3:T(8,128)} %copy.156), calls=%async_computation.5 | async-start | bytes 4194304 | tf_op jit(solution)/shard_map/all_to_all | solution.py:91
  107.7 4.7 %fusion.35 = (f32[32,256,64]{1,0,2:T(8,128)S(1)}, f32[32,256,64]{1,0,2:T(8,128)S(1)}, f32[32,256,64]{1,0,2:T(8,128)S(1)}, f32[32,256,64]{1,0,2:T(8,128)S(1)}) fusion(f32[32,256,64]{1,0,2:T(8,128)} %fusion.134, f32[32,256]{1,0:T(8,128)S(1)} %get-tuple-element.35, f32[32,256]{1,0:T(8,128)S(1)} %get-tuple-element.36, f32[32,256,64]{1,0,2:T(8,128)} %fusion.137, ...), kind=kOutput, calls=%fused_computation.59 | convolution fusion | flops 108010496 | bytes 15269888 | tf_op jit(solution)/shard_map/ja,bach->bjch/dot_general | solution.py:29
  112.4 3.8 fusion.52
  116.2 3.8 fusion.50
  120.0 4.0 fusion.42
  124.0 3.8 fusion.44
  127.8 3.9 fusion.58
  131.7 4.2 %fusion.61 = f32[32,64,256]{2,1,0:T(8,128)S(1)} fusion(f32[32,64,256]{2,1,0:T(8,128)S(1)} %fusion.50, f32[32,256,64]{1,0,2:T(8,128)S(1)} %get-tuple-element.29), kind=kOutput, calls=%fused_computation.88 | convolution fusion | flops 1612054528 | bytes 6291456 | tf_op jit(solution)/shard_map/cm,bjch->bjmh/dot_general | solution.py:42
  135.9 3.8 fusion.67
  139.7 4.1 %fusion.26 = (f32[1,32,256,64]{2,3,1,0:T(8,128)S(1)}, f32[1,32,256,64]{2,3,1,0:T(8,128)S(1)}) fusion(f32[32,64,256]{2,1,0:T(8,128)S(1)} %fusion.61, f32[32,64,256]{2,1,0:T(8,128)S(1)} %fusion.67, f32[32,64,256]{2,1,0:T(8,128)S(1)} %fusion.58, f32[32,64,256]{2,1,0:T(8,128)S(1)} %fusion.44, f32[32,256,64]{1,0,2:T(8,128)S(1)} %get-tuple-element.34), kind=kOutput, calls=%fused_computation.38 | convolution fusion | flops 1615200256 | bytes 14680064 | tf_op jit(solution)/shard_map/cm,bjch->bjmh/dot_general | solution.py:37
  145.8 2.9 copy.133
  148.7 3.2 copy.134
  151.9 7.6 %all-to-all-start = ((f32[2,2,256,16,32]{2,4,1,0,3:T(8,128)}), f32[2,2,256,16,32]{2,4,1,0,3:T(8,128)}, u32[]{:S(2)}, u32[]{:S(2)}) async-start(f32[2,2,256,16,32]{2,4,1,0,3:T(8,128)} %copy.134), calls=%async_computation | async-start | bytes 4194304 | tf_op jit(solution)/shard_map/all_to_all | solution.py:85
  166.1 34.5 %all-to-all-done = f32[2,2,256,16,32]{2,4,1,0,3:T(8,128)} async-done(((f32[2,2,256,16,32]{2,4,1,0,3:T(8,128)}), f32[2,2,256,16,32]{2,4,1,0,3:T(8,128)}, u32[]{:S(2)}, u32[]{:S(2)}) %all-to-all-start) | async-done | bytes 2097184 | tf_op jit(solution)/shard_map/all_to_all | solution.py:85
  200.5 3.2 copy.135
  203.7 6.5 %multiply_subtract_fusion = (f32[2,32,256,1,32]{2,4,1,0,3:T(8,128)S(1)}, f32[2,32,256,1,32]{2,4,1,0,3:T(8,128)}, f32[2,32,256,1,32]{2,4,1,0,3:T(8,128)}) fusion(f32[2,32,256,1,32]{2,4,1,0,3:T(8,128)} %bitcast.283, f32[2,32,256,1,32]{2,4,1,0,3:T(8,128)} %bitcast.281, bf16[2,32,256,1,32]{2,4,1,0,3:T(8,128)(2,1)} %reduce-scatter.2.cloned.1.call-done, ...), kind=kLoop, calls=%fused_computation.68 | loop fusion | flops 5242880 | bytes 13631488 | tf_op jit(solution)/shard_map/sub | solution.py:121
  211.7 11.3 %all-to-all-start.5 = ((f32[2,32,256,1,32]{2,4,0,3,1:T(8,128)}), f32[2,32,256,1,32]{2,4,0,3,1:T(8,128)}, u32[]{:S(2)}, u32[]{:S(2)}) async-start(f32[2,32,256,1,32]{2,4,0,3,1:T(8,128)} %copy.158), calls=%async_computation.6 | async-start | bytes 4194304 | tf_op jit(solution)/shard_map/all_to_all | solution.py:133
  223.0 3.2 copy.161
  226.2 37.8 %all-to-all-done.5 = f32[2,32,256,1,32]{2,4,0,3,1:T(8,128)} async-done(((f32[2,32,256,1,32]{2,4,0,3,1:T(8,128)}), f32[2,32,256,1,32]{2,4,0,3,1:T(8,128)}, u32[]{:S(2)}, u32[]{:S(2)}) %all-to-all-start.5) | async-done | bytes 2097184 | tf_op jit(solution)/shard_map/all_to_all | solution.py:133
  264.0 11.3 %all-to-all-start.6 = ((f32[2,32,256,1,32]{2,4,0,3,1:T(8,128)}), f32[2,32,256,1,32]{2,4,0,3,1:T(8,128)}, u32[]{:S(2)}, u32[]{:S(2)}) async-start(f32[2,32,256,1,32]{2,4,0,3,1:T(8,128)} %copy.161), calls=%async_computation.7 | async-start | bytes 4194304 | tf_op jit(solution)/shard_map/all_to_all | solution.py:136
  275.4 5.5 %fusion.8 = f32[2,32,256,32]{2,3,1,0:T(8,128)} fusion(f32[2,32,256,32]{2,3,1,0:T(8,128)} %bitcast.284, f32[2,32,256,32]{2,3,1,0:T(8,128)} %bitcast.280, bf16[2,32,256,1,32]{2,4,1,0,3:T(8,128)(2,1)S(1)} %copy-done.2, f32[2,32,256,32]{2,3,1,0:T(8,128)} %bitcast.282), kind=kLoop, calls=%fused_computation.14 | loop fusion | flops 5242880 | bytes 9437184 | tf_op jit(solution)/shard_map/sub | solution.py:121
  280.9 3.2 copy.164
  284.0 32.3 %all-to-all-done.6 = f32[2,32,256,1,32]{2,4,0,3,1:T(8,128)} async-done(((f32[2,32,256,1,32]{2,4,0,3,1:T(8,128)}), f32[2,32,256,1,32]{2,4,0,3,1:T(8,128)}, u32[]{:S(2)}, u32[]{:S(2)}) %all-to-all-start.6) | async-done | bytes 2097184 | tf_op jit(solution)/shard_map/all_to_all | solution.py:136
  316.3 11.4 %all-to-all-start.7 = ((f32[2,32,256,1,32]{2,4,0,3,1:T(8,128)}), f32[2,32,256,1,32]{2,4,0,3,1:T(8,128)}, u32[]{:S(2)}, u32[]{:S(2)}) async-start(f32[2,32,256,1,32]{2,4,0,3,1:T(8,128)} %copy.164), calls=%async_computation.8 | async-start | bytes 4194304 | tf_op jit(solution)/shard_map/all_to_all | solution.py:139
  327.8 11.3 %all-gather.2.cloned.1.call-done = f32[2,32,256,64]{2,3,1,0:T(8,128)} async-done(((f32[2,32,256,32]{2,3,1,0:T(8,128)}), f32[2,32,256,64]{2,3,1,0:T(8,128)}) %all-gather.2.cloned.1.call-update) | async-done | bytes 4194320 | tf_op jit(solution)/shard_map/all_gather | solution.py:122
  339.0 3.7 fusion.28
  342.8 2.8 fusion.20
  345.6 2.8 fusion.18
  348.5 2.9 fusion.70
  351.4 3.4 fusion.15
  354.8 2.4 fusion.38
  357.3 2.5 fusion.85
  360.0 2.8 copy.172
  362.8 2.7 reshape.247
  365.4 3.2 all-to-all-done.7
  368.6 11.2 %all-to-all-start.8 = ((bf16[16,2,8192]{2,1,0:T(2,128)(2,1)}), bf16[16,2,8192]{2,1,0:T(2,128)(2,1)S(1)}, u32[]{:S(2)}, u32[]{:S(2)}) async-start(bf16[16,2,8192]{2,1,0:T(2,128)(2,1)} %reshape.247), calls=%async_computation.9 | async-start | bytes 1048576 | tf_op jit(solution)/shard_map/all_to_all | solution.py:143
  390.9 3.2 all-to-all-done.8
  (42 shorter events, 34.0 us)
Async XLA Ops:
  7.2 9.5 %copy-start.3 = (bf16[1,256,1024]{2,1,0:T(8,128)(2,1)S(1)}, bf16[1,256,1024]{2,1,0:T(8,128)(2,1)}, u32[]{:S(2)}) copy-start(bf16[1,256,1024]{2,1,0:T(8,128)(2,1)} %param.5) | copy-start | bytes 1572868
  9.3 21.7 %all-to-all-start.3 = ((bf16[1,256,2,16,32]{1,4,2,0,3:T(8,128)(2,1)}), bf16[1,256,2,16,32]{1,4,2,0,3:T(8,128)(2,1)S(1)}, u32[]{:S(2)}, u32[]{:S(2)}) async-start(bf16[1,256,2,16,32]{1,4,2,0,3:T(8,128)(2,1)} %copy.145), calls=%async_computation.3 | async-start | bytes 1048576 | tf_op jit(solution)/shard_map/all_to_all | solution.py:81
  31.0 18.4 %all-to-all-start.2 = ((bf16[1,256,2,16,32]{1,4,2,0,3:T(8,128)(2,1)}), bf16[1,256,2,16,32]{1,4,2,0,3:T(8,128)(2,1)S(1)}, u32[]{:S(2)}, u32[]{:S(2)}) async-start(bf16[1,256,2,16,32]{1,4,2,0,3:T(8,128)(2,1)} %copy.140), calls=%async_computation.2 | async-start | bytes 1048576 | tf_op jit(solution)/shard_map/all_to_all | solution.py:80
  49.4 45.1 %all-to-all-start.1 = ((f32[2,2,256,16,32]{2,4,1,0,3:T(8,128)}), f32[2,2,256,16,32]{2,4,1,0,3:T(8,128)S(1)}, u32[]{:S(2)}, u32[]{:S(2)}) async-start(f32[2,2,256,16,32]{2,4,1,0,3:T(8,128)} %copy.137), calls=%async_computation.1 | async-start | bytes 4194304 | tf_op jit(solution)/shard_map/all_to_all | solution.py:88
  94.6 1.3 copy-start.1
  95.9 56.0 %all-to-all-start.4 = ((f32[2,2,256,16,32]{2,4,1,0,3:T(8,128)}), f32[2,2,256,16,32]{2,4,1,0,3:T(8,128)}, u32[]{:S(2)}, u32[]{:S(2)}) async-start(f32[2,2,256,16,32]{2,4,1,0,3:T(8,128)} %copy.156), calls=%async_computation.5 | async-start | bytes 4194304 | tf_op jit(solution)/shard_map/all_to_all | solution.py:91
  107.2 96.5 %reduce-scatter.2.cloned.1.call-start = ((), (), s32[]{:S(2)}) async-start(), calls=%async_computation.10 | async-start | bytes 3145728 | tf_op jit(solution)/shard_map/reduce_scatter | solution.py:115
  135.9 3.8 copy-start
  151.9 48.6 %all-to-all-start = ((f32[2,2,256,16,32]{2,4,1,0,3:T(8,128)}), f32[2,2,256,16,32]{2,4,1,0,3:T(8,128)}, u32[]{:S(2)}, u32[]{:S(2)}) async-start(f32[2,2,256,16,32]{2,4,1,0,3:T(8,128)} %copy.134), calls=%async_computation | async-start | bytes 4194304 | tf_op jit(solution)/shard_map/all_to_all | solution.py:85
  211.7 52.3 %all-to-all-start.5 = ((f32[2,32,256,1,32]{2,4,0,3,1:T(8,128)}), f32[2,32,256,1,32]{2,4,0,3,1:T(8,128)}, u32[]{:S(2)}, u32[]{:S(2)}) async-start(f32[2,32,256,1,32]{2,4,0,3,1:T(8,128)} %copy.158), calls=%async_computation.6 | async-start | bytes 4194304 | tf_op jit(solution)/shard_map/all_to_all | solution.py:133
  226.2 49.2 %copy-start.2 = (bf16[2,32,256,1,32]{2,4,1,0,3:T(8,128)(2,1)S(1)}, bf16[2,32,256,1,32]{2,4,1,0,3:T(8,128)(2,1)}, u32[]{:S(2)}) copy-start(bf16[2,32,256,1,32]{2,4,1,0,3:T(8,128)(2,1)} %reduce-scatter.2.cloned.1.call-done) | copy-start | bytes 3145732
  264.0 52.3 %all-to-all-start.6 = ((f32[2,32,256,1,32]{2,4,0,3,1:T(8,128)}), f32[2,32,256,1,32]{2,4,0,3,1:T(8,128)}, u32[]{:S(2)}, u32[]{:S(2)}) async-start(f32[2,32,256,1,32]{2,4,0,3,1:T(8,128)} %copy.161), calls=%async_computation.7 | async-start | bytes 4194304 | tf_op jit(solution)/shard_map/all_to_all | solution.py:136
  275.3 63.7 %all-gather.2.cloned.1.call-start = ((), (), s32[]{:S(2)}) async-start(), calls=%async_computation.11 | async-start | bytes 6291456 | tf_op jit(solution)/shard_map/all_gather | solution.py:122
  316.3 52.3 %all-to-all-start.7 = ((f32[2,32,256,1,32]{2,4,0,3,1:T(8,128)}), f32[2,32,256,1,32]{2,4,0,3,1:T(8,128)}, u32[]{:S(2)}, u32[]{:S(2)}) async-start(f32[2,32,256,1,32]{2,4,0,3,1:T(8,128)} %copy.164), calls=%async_computation.8 | async-start | bytes 4194304 | tf_op jit(solution)/shard_map/all_to_all | solution.py:139
  368.6 25.5 %all-to-all-start.8 = ((bf16[16,2,8192]{2,1,0:T(2,128)(2,1)}), bf16[16,2,8192]{2,1,0:T(2,128)(2,1)S(1)}, u32[]{:S(2)}, u32[]{:S(2)}) async-start(bf16[16,2,8192]{2,1,0:T(2,128)(2,1)} %reshape.247), calls=%async_computation.9 | async-start | bytes 1048576 | tf_op jit(solution)/shard_map/all_to_all | solution.py:143
Sparse Core Ops, SparseCore 0:
  145.9 33.1 reduce-scatter.1
  281.0 58.0 all-gather.1
where the time goes:
time: 410 us; the launch traced here: 405 us
  waiting for transfers between devices  173 us (42%)
  starting transfers between devices  80.3 us (20%)
  matrix products  60.2 us (15%)
  local copies, waits for them, and re-layouts  54.6 us (13%)
  other arithmetic  21.5 us (5%)
  between operations  14.6 us (4%)
    all_to_all x1, waiting for transfers between devices, channel_layout(): lax.all_to_all(new_spectrum.reshape(back_shape), 'seq', split_axis=1, con...  37.8 us
    all_to_all x1, waiting for transfers between devices, channel_layout(): lax.all_to_all(spectrum.reshape(state_shape), 'seq', split_axis=3, concat...  34.5 us
    all_to_all x1, waiting for transfers between devices, channel_layout(): lax.all_to_all(new_first.reshape(back_shape), 'seq', split_axis=1, concat...  32.3 us
    all_to_all x1, waiting for transfers between devices, channel_layout(): lax.all_to_all(first_moment.reshape(state_shape), 'seq', split_axis=3, co...  26.9 us
    unnamed x19, local copies, waits for them, and re-layouts  20.7 us
    all_to_all x1, waiting for transfers between devices, channel_layout(): lax.all_to_all(cotangent_parts, 'seq', split_axis=3, concat_axis=1, tiled...  13.2 us
    sub x2, other arithmetic, channel_layout(): spec_cols - step_rate * jnp.tanh(new_first / (jnp.sqrt(new_second) + epsi...  12 us
    all_to_all x1, starting transfers between devices, channel_layout(): lax.all_to_all(new_second.reshape(back_shape), 'seq', split_axis=1, conca...  11.4 us
  transfers between devices with their start and end apart: 11, of which 9 were waited for; matrix products, arithmetic and copies ran while one was open for 30% of the time, Pallas kernels for 0%

commit v1 on v0

--- a/solution.py
+++ b/solution.py
@@ -7,6 +7,29 @@
 full_turn = 2.0 * math.pi
 step_rate = 0.5
 epsilon = 1e-06
+
+
+def split_up(array, dim, peers):
+    shape = array.shape
+    pieces = array.reshape(*shape[:dim], peers, shape[dim] // peers, *shape[dim + 1 :])
+    return jnp.moveaxis(pieces, dim, 0)
+
+
+def laid_out(parts, dim):
+    lengths = list(parts.shape[1:])
+    lengths[dim] *= parts.shape[0]
+    return jnp.moveaxis(parts, 0, dim).reshape(lengths)
+
+
+def sent_to_each(x, axis, split_dim, concat_dim):
+    length, index = (lax.axis_size(axis), lax.axis_index(axis))
+    pieces = split_up(x, split_dim, length)
+    outs = [pieces[index]]
+    for hop in range(1, length):
+        sent = pieces[(index + hop) % length]
+        outs.append(lax.ppermute(sent, axis, [(i, (i + hop) % length) for i in range(length)]))
+    pieces = jnp.stack(outs)[(index - jnp.arange(length)) % length]
+    return laid_out(pieces, concat_dim)
 
 
 def angles(numer, modulus):
@@ -133,9 +156,7 @@
         lax.all_to_all(
             new_spectrum.reshape(back_shape), "seq", split_axis=1, concat_axis=3, tiled=True
         ),
-        lax.all_to_all(
-            new_first.reshape(back_shape), "seq", split_axis=1, concat_axis=3, tiled=True
-        ),
+        sent_to_each(new_first.reshape(back_shape), "seq", 1, 3),
         lax.all_to_all(
             new_second.reshape(back_shape), "seq", split_axis=1, concat_axis=3, tiled=True
         ),

time: 410 us -> 441 us (1.076)
  starting transfers between devices: 80.3 us -> 131 us
  waiting for transfers between devices: 173 us -> 130 us
  local copies, waits for them, and re-layouts: 54.6 us -> 75.6 us
    ppermute x0 -> x15, starting transfers between devices: none -> 67.3 us  [sent_to_each(): lax.ppermute(sent, axis, [(i, (i + hop) % length) for i in range(length)])]
    ppermute x0 -> x15, waiting for transfers between devices: none -> 43.2 us  [sent_to_each(): lax.ppermute(sent, axis, [(i, (i + hop) % length) for i in range(length)])]
    all_to_all x1, waiting for transfers between devices: 37.8 us -> 0.01 us  [channel_layout(): lax.all_to_all(new_spectrum.reshape(back_shape), 'seq', split_axis=1, con...]
    all_to_all x1 -> x0, waiting for transfers between devices: 32.3 us -> none  [channel_layout(): lax.all_to_all(new_first.reshape(back_shape), 'seq', split_axis=1, concat...]
    unnamed x19 -> x42, local copies, waits for them, and re-layouts: 20.7 us -> 38.3 us
    all_to_all x1 -> x0, starting transfers between devices: 11.3 us -> none  [channel_layout(): lax.all_to_all(new_first.reshape(back_shape), 'seq', split_axis=1, concat...]
    all_gather x1, waiting for transfers between devices: 11.3 us -> 0.02 us  [channel_layout(): group_filter = lax.all_gather(new_spectrum, 'batch', axis=3, tiled=True)]
    add x0 -> x2, other arithmetic: none -> 8.6 us  [the longest x1 6.54 us: channel_layout(): new_second = 0.99 * second_cols + 0.01 * own_grad * own_grad]
  transfers between devices with their start and end apart: 11 -> 25, of which waited for: 9 -> 7; matrix products, arithmetic and copies ran while one was open for 30% -> 33% of each run, Pallas kernels for 0% -> 0%
where the time goes in v1:
time: 441 us; the launch traced here: 435 us
  starting transfers between devices  131 us (30%)
  waiting for transfers between devices  130 us (29%)
  local copies, waits for them, and re-layouts  75.6 us (17%)
  matrix products  59.9 us (14%)
  other arithmetic  22.7 us (5%)
  between operations  15 us (3%)
    ppermute x15, starting transfers between devices, sent_to_each(): lax.ppermute(sent, axis, [(i, (i + hop) % length) for i in range(length)])  67.3 us
    ppermute x15, waiting for transfers between devices, sent_to_each(): lax.ppermute(sent, axis, [(i, (i + hop) % length) for i in range(length)])  43.2 us
    unnamed x42, local copies, waits for them, and re-layouts  38.3 us
    all_to_all x1, waiting for transfers between devices, channel_layout(): lax.all_to_all(spectrum.reshape(state_shape), 'seq', split_axis=3, concat...  35.9 us
    all_to_all x1, waiting for transfers between devices, channel_layout(): lax.all_to_all(first_moment.reshape(state_shape), 'seq', split_axis=3, co...  27 us
    all_to_all x1, starting transfers between devices, channel_layout(): lax.all_to_all(new_second.reshape(back_shape), 'seq', split_axis=1, conca...  13.4 us
    all_to_all x1, waiting for transfers between devices, channel_layout(): lax.all_to_all(cotangent_parts, 'seq', split_axis=3, concat_axis=1, tiled...  13.2 us
    all_to_all x1, starting transfers between devices, channel_layout(): lax.all_to_all(new_spectrum.reshape(back_shape), 'seq', split_axis=1, con...  11.4 us
  transfers between devices with their start and end apart: 25, of which 7 were waited for; matrix products, arithmetic and copies ran while one was open for 33% of the time, Pallas kernels for 0%

profile of v1, /device:TPU:0, one launch (start us, length us, event | category | flops | bytes accessed | tf_op | source)
XLA Modules:
  0.0 434.9 jit_solution(91584089899371282)
XLA Ops:
  9.3 7.4 %all-to-all-start.3 = ((bf16[1,256,2,16,32]{1,4,2,0,3:T(8,128)(2,1)}), bf16[1,256,2,16,32]{1,4,2,0,3:T(8,128)(2,1)S(1)}, u32[]{:S(2)}, u32[]{:S(2)}) async-start(bf16[1,256,2,16,32]{1,4,2,0,3:T(8,128)(2,1)} %copy.147), calls=%async_computation.3 | async-start | bytes 1048576 | tf_op jit(solution)/shard_map/all_to_all | solution.py:104
  17.8 13.2 %all-to-all-done.3 = bf16[1,256,2,16,32]{1,4,2,0,3:T(8,128)(2,1)S(1)} async-done(((bf16[1,256,2,16,32]{1,4,2,0,3:T(8,128)(2,1)}), bf16[1,256,2,16,32]{1,4,2,0,3:T(8,128)(2,1)S(1)}, u32[]{:S(2)}, u32[]{:S(2)}) %all-to-all-start.3) | async-done | bytes 524320 | tf_op jit(solution)/shard_map/all_to_all | solution.py:104
  31.0 4.2 all-to-all-start.2
  38.7 10.8 %all-to-all-done.2 = bf16[1,256,2,16,32]{1,4,2,0,3:T(8,128)(2,1)S(1)} async-done(((bf16[1,256,2,16,32]{1,4,2,0,3:T(8,128)(2,1)}), bf16[1,256,2,16,32]{1,4,2,0,3:T(8,128)(2,1)S(1)}, u32[]{:S(2)}, u32[]{:S(2)}) %all-to-all-start.2) | async-done | bytes 524320 | tf_op jit(solution)/shard_map/all_to_all | solution.py:103
  49.4 4.2 all-to-all-start.1
  53.6 2.9 copy.157
  56.5 3.2 copy.158
  60.4 2.4 fusion.131
  62.8 2.4 fusion.136
  67.6 27.0 %all-to-all-done.1 = f32[2,2,256,16,32]{2,4,1,0,3:T(8,128)S(1)} async-done(((f32[2,2,256,16,32]{2,4,1,0,3:T(8,128)}), f32[2,2,256,16,32]{2,4,1,0,3:T(8,128)S(1)}, u32[]{:S(2)}, u32[]{:S(2)}) %all-to-all-start.1) | async-done | bytes 2097184 | tf_op jit(solution)/shard_map/all_to_all | solution.py:111
  94.6 11.3 %all-to-all-start.4 = ((f32[2,2,256,16,32]{2,4,1,0,3:T(8,128)}), f32[2,2,256,16,32]{2,4,1,0,3:T(8,128)}, u32[]{:S(2)}, u32[]{:S(2)}) async-start(f32[2,2,256,16,32]{2,4,1,0,3:T(8,128)} %copy.158), calls=%async_computation.5 | async-start | bytes 4194304 | tf_op jit(solution)/shard_map/all_to_all | solution.py:114
  106.4 4.7 %fusion.34 = (f32[32,256,64]{1,0,2:T(8,128)S(1)}, f32[32,256,64]{1,0,2:T(8,128)S(1)}, f32[32,256,64]{1,0,2:T(8,128)S(1)}, f32[32,256,64]{1,0,2:T(8,128)S(1)}) fusion(f32[32,256,64]{1,0,2:T(8,128)} %fusion.133, f32[32,256]{1,0:T(8,128)S(1)} %get-tuple-element.50, f32[32,256]{1,0:T(8,128)S(1)} %get-tuple-element.51, f32[32,256,64]{1,0,2:T(8,128)} %fusion.136, ...), kind=kOutput, calls=%fused_computation.59 | convolution fusion | flops 108010496 | bytes 15269888 | tf_op jit(solution)/shard_map/ja,bach->bjch/dot_general | solution.py:52
  111.1 3.8 fusion.51
  114.9 3.8 fusion.49
  118.7 4.0 fusion.41
  122.7 3.8 fusion.43
  126.5 3.9 fusion.57
  130.3 4.0 fusion.60
  134.4 3.8 fusion.66
  138.2 4.1 fusion.25
  144.2 2.9 copy.135
  147.1 3.2 copy.136
  150.3 8.2 %all-to-all-start = ((f32[2,2,256,16,32]{2,4,1,0,3:T(8,128)}), f32[2,2,256,16,32]{2,4,1,0,3:T(8,128)}, u32[]{:S(2)}, u32[]{:S(2)}) async-start(f32[2,2,256,16,32]{2,4,1,0,3:T(8,128)} %copy.136), calls=%async_computation | async-start | bytes 4194304 | tf_op jit(solution)/shard_map/all_to_all | solution.py:108
  163.7 35.9 %all-to-all-done = f32[2,2,256,16,32]{2,4,1,0,3:T(8,128)} async-done(((f32[2,2,256,16,32]{2,4,1,0,3:T(8,128)}), f32[2,2,256,16,32]{2,4,1,0,3:T(8,128)}, u32[]{:S(2)}, u32[]{:S(2)}) %all-to-all-start) | async-done | bytes 2097184 | tf_op jit(solution)/shard_map/all_to_all | solution.py:108
  199.6 3.2 copy.137
  202.7 6.5 %fusion.12 = (f32[2,32,256,1,32]{2,4,1,0,3:T(8,128)}, f32[2,32,256,1,32]{2,4,1,0,3:T(8,128)S(1)}, f32[2,32,256,1,32]{2,4,1,0,3:T(8,128)}) fusion(f32[2,32,256,1,32]{2,4,1,0,3:T(8,128)} %bitcast.351, bf16[2,32,256,1,32]{2,4,1,0,3:T(8,128)(2,1)} %reduce-scatter.2.cloned.1.call-done, f32[2,32,256,1,32]{2,4,1,0,3:T(8,128)} %bitcast.353, ...), kind=kLoop, calls=%fused_computation.19 | loop fusion | flops 5242880 | bytes 13631488 | tf_op jit(solution)/shard_map/add | solution.py:143
  210.7 11.4 %all-to-all-start.5 = ((f32[2,32,256,1,32]{2,4,0,3,1:T(8,128)}), f32[2,32,256,1,32]{2,4,0,3,1:T(8,128)}, u32[]{:S(2)}, u32[]{:S(2)}) async-start(f32[2,32,256,1,32]{2,4,0,3,1:T(8,128)} %copy.160), calls=%async_computation.6 | async-start | bytes 4194304 | tf_op jit(solution)/shard_map/all_to_all | solution.py:156
  222.2 5.6 %fusion.8 = f32[2,32,256,32]{2,3,1,0:T(8,128)} fusion(f32[2,32,256,32]{2,3,1,0:T(8,128)} %bitcast.354, f32[2,32,256,32]{2,3,1,0:T(8,128)} %bitcast.350, bf16[2,32,256,1,32]{2,4,1,0,3:T(8,128)(2,1)S(1)} %copy-done.5, f32[2,32,256,32]{2,3,1,0:T(8,128)} %bitcast.352), kind=kLoop, calls=%fused_computation.15 | loop fusion | flops 5242880 | bytes 9437184 | tf_op jit(solution)/shard_map/sub | solution.py:144
  240.7 23.6 %collective-permute-done = f32[2,2,256,1,32]{2,4,1,0,3:T(8,128)} collective-permute-done((f32[2,2,256,1,32]{2,4,1,0,3:T(8,128)}, f32[2,2,256,1,32]{2,4,1,0,3:T(8,128)}, u32[]{:S(2)}, u32[]{:S(2)}) %collective-permute-start) | collective-permute-done | bytes 131104 | tf_op jit(solution)/shard_map/ppermute | solution.py:30
  265.3 14.5 %collective-permute-start.6 = (f32[2,2,256,1,32]{2,4,1,0,3:T(8,128)S(1)}, f32[2,2,256,1,32]{2,4,1,0,3:T(8,128)}, u32[]{:S(2)}, u32[]{:S(2)}) collective-permute-start(f32[2,2,256,1,32]{2,4,1,0,3:T(8,128)S(1)} %get-tuple-element.40), channel_id=1, source_target_pairs={{0,14},{2,16},{4,18},{6,20},{8,22},{10,24},{12,26},{14,28},{16,30}... | collective-permute-start | bytes 393224 | tf_op jit(solution)/shard_map/ppermute | solution.py:30
  283.3 13.4 %all-to-all-start.6 = ((f32[2,32,256,1,32]{2,4,0,3,1:T(8,128)}), f32[2,32,256,1,32]{2,4,0,3,1:T(8,128)}, u32[]{:S(2)}, u32[]{:S(2)}) async-start(f32[2,32,256,1,32]{2,4,0,3,1:T(8,128)} %copy.165), calls=%async_computation.7 | async-start | bytes 4194304 | tf_op jit(solution)/shard_map/all_to_all | solution.py:160
  297.7 3.7 collective-permute-start.9
  308.2 8.8 %collective-permute-start.13 = (f32[2,2,256,1,32]{2,4,1,0,3:T(8,128)S(1)}, f32[2,2,256,1,32]{2,4,1,0,3:T(8,128)}, u32[]{:S(2)}, u32[]{:S(2)}) collective-permute-start(f32[2,2,256,1,32]{2,4,1,0,3:T(8,128)S(1)} %get-tuple-element.33), channel_id=1, source_target_pairs={{0,28},{2,30},{4,0},{6,2},{8,4},{10,6},{12,8},{14,10},{16,12},{18,... | collective-permute-start | bytes 393224 | tf_op jit(solution)/shard_map/ppermute | solution.py:30
  317.0 19.5 %collective-permute-done.9 = f32[2,2,256,1,32]{2,4,1,0,3:T(8,128)S(1)} collective-permute-done((f32[2,2,256,1,32]{2,4,1,0,3:T(8,128)S(1)}, f32[2,2,256,1,32]{2,4,1,0,3:T(8,128)S(1)}, u32[]{:S(2)}, u32[]{:S(2)}) %collective-permute-start.9) | collective-permute-done | bytes 131104 | tf_op jit(solution)/shard_map/ppermute | solution.py:30
  336.5 27.7 %collective-permute-start.14 = (f32[2,2,256,1,32]{2,4,1,0,3:T(8,128)S(1)}, f32[2,2,256,1,32]{2,4,1,0,3:T(8,128)}, u32[]{:S(2)}, u32[]{:S(2)}) collective-permute-start(f32[2,2,256,1,32]{2,4,1,0,3:T(8,128)S(1)} %get-tuple-element.32), channel_id=1, source_target_pairs={{0,30},{2,0},{4,2},{6,4},{8,6},{10,8},{12,10},{14,12},{16,14},{18,... | collective-permute-start | bytes 393224 | tf_op jit(solution)/shard_map/ppermute | solution.py:30
  364.3 4.3 fusion.27
  368.6 2.8 fusion.19
  371.5 2.8 fusion.17
  374.3 2.9 fusion.69
  377.2 3.4 fusion.14
  380.7 2.4 fusion.37
  383.1 2.5 fusion.84
  385.8 3.8 copy.173
  389.7 5.9 %reshape.344 = bf16[16,2,8192]{2,1,0:T(2,128)(2,1)} reshape(bf16[4096,1,1,2,32]{4,3,2,1,0:T(2,128)(2,1)} %bitcast.357) | data formatting | bytes 1048576
  395.6 3.6 all-to-all-start.7
  409.0 2.9 copy.177
  415.2 2.9 copy.176
  421.6 2.9 copy.178
  (97 shorter events, 64.0 us)
Async XLA Ops:
  7.2 9.5 %copy-start.6 = (bf16[1,256,1024]{2,1,0:T(8,128)(2,1)S(1)}, bf16[1,256,1024]{2,1,0:T(8,128)(2,1)}, u32[]{:S(2)}) copy-start(bf16[1,256,1024]{2,1,0:T(8,128)(2,1)} %param.5) | copy-start | bytes 1572868
  9.3 21.7 %all-to-all-start.3 = ((bf16[1,256,2,16,32]{1,4,2,0,3:T(8,128)(2,1)}), bf16[1,256,2,16,32]{1,4,2,0,3:T(8,128)(2,1)S(1)}, u32[]{:S(2)}, u32[]{:S(2)}) async-start(bf16[1,256,2,16,32]{1,4,2,0,3:T(8,128)(2,1)} %copy.147), calls=%async_computation.3 | async-start | bytes 1048576 | tf_op jit(solution)/shard_map/all_to_all | solution.py:104
  31.0 18.4 %all-to-all-start.2 = ((bf16[1,256,2,16,32]{1,4,2,0,3:T(8,128)(2,1)}), bf16[1,256,2,16,32]{1,4,2,0,3:T(8,128)(2,1)S(1)}, u32[]{:S(2)}, u32[]{:S(2)}) async-start(bf16[1,256,2,16,32]{1,4,2,0,3:T(8,128)(2,1)} %copy.142), calls=%async_computation.2 | async-start | bytes 1048576 | tf_op jit(solution)/shard_map/all_to_all | solution.py:103
  49.4 45.1 %all-to-all-start.1 = ((f32[2,2,256,16,32]{2,4,1,0,3:T(8,128)}), f32[2,2,256,16,32]{2,4,1,0,3:T(8,128)S(1)}, u32[]{:S(2)}, u32[]{:S(2)}) async-start(f32[2,2,256,16,32]{2,4,1,0,3:T(8,128)} %copy.139), calls=%async_computation.1 | async-start | bytes 4194304 | tf_op jit(solution)/shard_map/all_to_all | solution.py:111
  94.6 55.8 %all-to-all-start.4 = ((f32[2,2,256,16,32]{2,4,1,0,3:T(8,128)}), f32[2,2,256,16,32]{2,4,1,0,3:T(8,128)}, u32[]{:S(2)}, u32[]{:S(2)}) async-start(f32[2,2,256,16,32]{2,4,1,0,3:T(8,128)} %copy.158), calls=%async_computation.5 | async-start | bytes 4194304 | tf_op jit(solution)/shard_map/all_to_all | solution.py:114
  105.8 96.9 %reduce-scatter.2.cloned.1.call-start = ((), (), s32[]{:S(2)}) async-start(), calls=%async_computation.9 | async-start | bytes 3145728 | tf_op jit(solution)/shard_map/reduce_scatter | solution.py:138
  130.3 7.8 %copy-start.1 = (f32[32,64,256]{2,1,0:T(8,128)}, f32[32,64,256]{2,1,0:T(8,128)S(1)}, u32[]{:S(2)}) copy-start(f32[32,64,256]{2,1,0:T(8,128)S(1)} %fusion.57) | copy-start | bytes 6291460
  134.3 3.8 copy-start.2
  150.3 49.2 %all-to-all-start = ((f32[2,2,256,16,32]{2,4,1,0,3:T(8,128)}), f32[2,2,256,16,32]{2,4,1,0,3:T(8,128)}, u32[]{:S(2)}, u32[]{:S(2)}) async-start(f32[2,2,256,16,32]{2,4,1,0,3:T(8,128)} %copy.136), calls=%async_computation | async-start | bytes 4194304 | tf_op jit(solution)/shard_map/all_to_all | solution.py:108
  210.7 11.5 %copy-start.5 = (bf16[2,32,256,1,32]{2,4,1,0,3:T(8,128)(2,1)S(1)}, bf16[2,32,256,1,32]{2,4,1,0,3:T(8,128)(2,1)}, u32[]{:S(2)}) copy-start(bf16[2,32,256,1,32]{2,4,1,0,3:T(8,128)(2,1)} %reduce-scatter.2.cloned.1.call-done) | copy-start | bytes 3145732
  210.7 72.6 %all-to-all-start.5 = ((f32[2,32,256,1,32]{2,4,0,3,1:T(8,128)}), f32[2,32,256,1,32]{2,4,0,3,1:T(8,128)}, u32[]{:S(2)}, u32[]{:S(2)}) async-start(f32[2,32,256,1,32]{2,4,0,3,1:T(8,128)} %copy.160), calls=%async_computation.6 | async-start | bytes 4194304 | tf_op jit(solution)/shard_map/all_to_all | solution.py:156
  222.1 142.2 %all-gather.2.cloned.1.call-start = ((), (), s32[]{:S(2)}) async-start(), calls=%async_computation.10 | async-start | bytes 6291456 | tf_op jit(solution)/shard_map/all_gather | solution.py:145
  230.1 1.3 copy-start.3
  231.4 6.8 %copy-start.4 = (f32[2,32,256,1,32]{2,4,1,0,3:T(8,128)S(1)}, f32[2,32,256,1,32]{2,4,1,0,3:T(8,128)}, u32[]{:S(2)}) copy-start(f32[2,32,256,1,32]{2,4,1,0,3:T(8,128)} %get-tuple-element.30) | copy-start | bytes 6291460
  232.3 31.9 %collective-permute-start = (f32[2,2,256,1,32]{2,4,1,0,3:T(8,128)}, f32[2,2,256,1,32]{2,4,1,0,3:T(8,128)}, u32[]{:S(2)}, u32[]{:S(2)}) collective-permute-start(f32[2,2,256,1,32]{2,4,1,0,3:T(8,128)} %get-tuple-element.46), channel_id=1, source_target_pairs={{0,2},{2,4},{4,6},{6,8},{8,10},{10,12},{12,14},{14,16},{16,18},{18... | collective-permute-start | bytes 393224 | tf_op jit(solution)/shard_map/ppermute | solution.py:30
  232.7 32.6 %collective-permute-start.1 = (f32[2,2,256,1,32]{2,4,1,0,3:T(8,128)}, f32[2,2,256,1,32]{2,4,1,0,3:T(8,128)S(1)}, u32[]{:S(2)}, u32[]{:S(2)}) collective-permute-start(f32[2,2,256,1,32]{2,4,1,0,3:T(8,128)} %get-tuple-element.45), channel_id=1, source_target_pairs={{0,4},{2,6},{4,8},{6,10},{8,12},{10,14},{12,16},{14,18},{16,20},{1... | collective-permute-start | bytes 393224 | tf_op jit(solution)/shard_map/ppermute | solution.py:30
  234.3 45.4 %collective-permute-start.2 = (f32[2,2,256,1,32]{2,4,1,0,3:T(8,128)S(1)}, f32[2,2,256,1,32]{2,4,1,0,3:T(8,128)S(1)}, u32[]{:S(2)}, u32[]{:S(2)}) collective-permute-start(f32[2,2,256,1,32]{2,4,1,0,3:T(8,128)S(1)} %get-tuple-element.44), channel_id=1, source_target_pairs={{0,6},{2,8},{4,10},{6,12},{8,14},{10,16},{12,18},{14,20},{16,22},{... | collective-permute-start | bytes 393224 | tf_op jit(solution)/shard_map/ppermute | solution.py:30
  236.6 43.7 %collective-permute-start.3 = (f32[2,2,256,1,32]{2,4,1,0,3:T(8,128)S(1)}, f32[2,2,256,1,32]{2,4,1,0,3:T(8,128)S(1)}, u32[]{:S(2)}, u32[]{:S(2)}) collective-permute-start(f32[2,2,256,1,32]{2,4,1,0,3:T(8,128)S(1)} %get-tuple-element.43), channel_id=1, source_target_pairs={{0,8},{2,10},{4,12},{6,14},{8,16},{10,18},{12,20},{14,22},{16,24},... | collective-permute-start | bytes 393224 | tf_op jit(solution)/shard_map/ppermute | solution.py:30
  238.1 59.6 %collective-permute-start.4 = (f32[2,2,256,1,32]{2,4,1,0,3:T(8,128)S(1)}, f32[2,2,256,1,32]{2,4,1,0,3:T(8,128)}, u32[]{:S(2)}, u32[]{:S(2)}) collective-permute-start(f32[2,2,256,1,32]{2,4,1,0,3:T(8,128)S(1)} %get-tuple-element.42), channel_id=1, source_target_pairs={{0,10},{2,12},{4,14},{6,16},{8,18},{10,20},{12,22},{14,24},{16,26}... | collective-permute-start | bytes 393224 | tf_op jit(solution)/shard_map/ppermute | solution.py:30
  264.2 38.1 %collective-permute-start.5 = (f32[2,2,256,1,32]{2,4,1,0,3:T(8,128)S(1)}, f32[2,2,256,1,32]{2,4,1,0,3:T(8,128)}, u32[]{:S(2)}, u32[]{:S(2)}) collective-permute-start(f32[2,2,256,1,32]{2,4,1,0,3:T(8,128)S(1)} %get-tuple-element.41), channel_id=1, source_target_pairs={{0,12},{2,14},{4,16},{6,18},{8,20},{10,22},{12,24},{14,26},{16,28}... | collective-permute-start | bytes 393224 | tf_op jit(solution)/shard_map/ppermute | solution.py:30
  265.3 38.0 %collective-permute-start.6 = (f32[2,2,256,1,32]{2,4,1,0,3:T(8,128)S(1)}, f32[2,2,256,1,32]{2,4,1,0,3:T(8,128)}, u32[]{:S(2)}, u32[]{:S(2)}) collective-permute-start(f32[2,2,256,1,32]{2,4,1,0,3:T(8,128)S(1)} %get-tuple-element.40), channel_id=1, source_target_pairs={{0,14},{2,16},{4,18},{6,20},{8,22},{10,24},{12,26},{14,28},{16,30}... | collective-permute-start | bytes 393224 | tf_op jit(solution)/shard_map/ppermute | solution.py:30
  279.8 26.6 %collective-permute-start.7 = (f32[2,2,256,1,32]{2,4,1,0,3:T(8,128)S(1)}, f32[2,2,256,1,32]{2,4,1,0,3:T(8,128)S(1)}, u32[]{:S(2)}, u32[]{:S(2)}) collective-permute-start(f32[2,2,256,1,32]{2,4,1,0,3:T(8,128)S(1)} %get-tuple-element.39), channel_id=1, source_target_pairs={{0,16},{2,18},{4,20},{6,22},{8,24},{10,26},{12,28},{14,30},{16,0},... | collective-permute-start | bytes 393224 | tf_op jit(solution)/shard_map/ppermute | solution.py:30
  280.3 0.7 copy-start.7
  281.0 27.2 %collective-permute-start.8 = (f32[2,2,256,1,32]{2,4,1,0,3:T(8,128)S(1)}, f32[2,2,256,1,32]{2,4,1,0,3:T(8,128)S(1)}, u32[]{:S(2)}, u32[]{:S(2)}) collective-permute-start(f32[2,2,256,1,32]{2,4,1,0,3:T(8,128)S(1)} %get-tuple-element.38), channel_id=1, source_target_pairs={{0,18},{2,20},{4,22},{6,24},{8,26},{10,28},{12,30},{14,0},{16,2},{... | collective-permute-start | bytes 393224 | tf_op jit(solution)/shard_map/ppermute | solution.py:30
  283.3 112.2 %all-to-all-start.6 = ((f32[2,32,256,1,32]{2,4,0,3,1:T(8,128)}), f32[2,32,256,1,32]{2,4,0,3,1:T(8,128)}, u32[]{:S(2)}, u32[]{:S(2)}) async-start(f32[2,32,256,1,32]{2,4,0,3,1:T(8,128)} %copy.165), calls=%async_computation.7 | async-start | bytes 4194304 | tf_op jit(solution)/shard_map/all_to_all | solution.py:160
  297.7 38.9 %collective-permute-start.9 = (f32[2,2,256,1,32]{2,4,1,0,3:T(8,128)S(1)}, f32[2,2,256,1,32]{2,4,1,0,3:T(8,128)S(1)}, u32[]{:S(2)}, u32[]{:S(2)}) collective-permute-start(f32[2,2,256,1,32]{2,4,1,0,3:T(8,128)S(1)} %get-tuple-element.37), channel_id=1, source_target_pairs={{0,20},{2,22},{4,24},{6,26},{8,28},{10,30},{12,0},{14,2},{16,4},{1... | collective-permute-start | bytes 393224 | tf_op jit(solution)/shard_map/ppermute | solution.py:30
  302.3 96.8 %collective-permute-start.10 = (f32[2,2,256,1,32]{2,4,1,0,3:T(8,128)}, f32[2,2,256,1,32]{2,4,1,0,3:T(8,128)}, u32[]{:S(2)}, u32[]{:S(2)}) collective-permute-start(f32[2,2,256,1,32]{2,4,1,0,3:T(8,128)} %get-tuple-element.36), channel_id=1, source_target_pairs={{0,22},{2,24},{4,26},{6,28},{8,30},{10,0},{12,2},{14,4},{16,6},{18... | collective-permute-start | bytes 393224 | tf_op jit(solution)/shard_map/ppermute | solution.py:30
  303.3 96.8 %collective-permute-start.11 = (f32[2,2,256,1,32]{2,4,1,0,3:T(8,128)}, f32[2,2,256,1,32]{2,4,1,0,3:T(8,128)}, u32[]{:S(2)}, u32[]{:S(2)}) collective-permute-start(f32[2,2,256,1,32]{2,4,1,0,3:T(8,128)} %get-tuple-element.35), channel_id=1, source_target_pairs={{0,24},{2,26},{4,28},{6,30},{8,0},{10,2},{12,4},{14,6},{16,8},{18,... | collective-permute-start | bytes 393224 | tf_op jit(solution)/shard_map/ppermute | solution.py:30
  306.4 94.6 %collective-permute-start.12 = (f32[2,2,256,1,32]{2,4,1,0,3:T(8,128)}, f32[2,2,256,1,32]{2,4,1,0,3:T(8,128)}, u32[]{:S(2)}, u32[]{:S(2)}) collective-permute-start(f32[2,2,256,1,32]{2,4,1,0,3:T(8,128)} %get-tuple-element.34), channel_id=1, source_target_pairs={{0,26},{2,28},{4,30},{6,0},{8,2},{10,4},{12,6},{14,8},{16,10},{18,... | collective-permute-start | bytes 393224 | tf_op jit(solution)/shard_map/ppermute | solution.py:30
  308.2 93.7 %collective-permute-start.13 = (f32[2,2,256,1,32]{2,4,1,0,3:T(8,128)S(1)}, f32[2,2,256,1,32]{2,4,1,0,3:T(8,128)}, u32[]{:S(2)}, u32[]{:S(2)}) collective-permute-start(f32[2,2,256,1,32]{2,4,1,0,3:T(8,128)S(1)} %get-tuple-element.33), channel_id=1, source_target_pairs={{0,28},{2,30},{4,0},{6,2},{8,4},{10,6},{12,8},{14,10},{16,12},{18,... | collective-permute-start | bytes 393224 | tf_op jit(solution)/shard_map/ppermute | solution.py:30
  336.5 66.3 %collective-permute-start.14 = (f32[2,2,256,1,32]{2,4,1,0,3:T(8,128)S(1)}, f32[2,2,256,1,32]{2,4,1,0,3:T(8,128)}, u32[]{:S(2)}, u32[]{:S(2)}) collective-permute-start(f32[2,2,256,1,32]{2,4,1,0,3:T(8,128)S(1)} %get-tuple-element.32), channel_id=1, source_target_pairs={{0,30},{2,0},{4,2},{6,4},{8,6},{10,8},{12,10},{14,12},{16,14},{18,... | collective-permute-start | bytes 393224 | tf_op jit(solution)/shard_map/ppermute | solution.py:30
  395.6 28.9 %all-to-all-start.7 = ((bf16[16,2,8192]{2,1,0:T(2,128)(2,1)}), bf16[16,2,8192]{2,1,0:T(2,128)(2,1)S(1)}, u32[]{:S(2)}, u32[]{:S(2)}) async-start(bf16[16,2,8192]{2,1,0:T(2,128)(2,1)} %reshape.344), calls=%async_computation.8 | async-start | bytes 1048576 | tf_op jit(solution)/shard_map/all_to_all | solution.py:164
  403.8 1.3 copy-start
Sparse Core Ops, SparseCore 0:
  144.4 33.1 reduce-scatter.1
  227.9 58.0 all-gather.1
